TPU v7x, 128 devices: a whole 4x4x4 slice. The times are simulated.
128 devices in a mesh: guide: 2 (over core), tensor: 16 (over y, x), batch: 4 (over z).
Axes of the slice: x: 4, y: 4, z: 4, core: 2. Of those that a mesh axis runs over, the one named last changes fastest.
Arguments:
- stream: bfloat16 [2, 512, 2048], P('guide', ('batch', 'tensor')), may hold values from -6 to 6
- attn_gain: float32 [2048], replicated, may hold values from 0.25 to 1.75
- w_qkv: bfloat16 [2048, 3072], P(None, 'tensor'), may hold values from -0.125 to 0.125
- cache_keys: bfloat16 [2, 512, 1024, 512], P('guide', ('batch', 'tensor')), may hold values from -600 to 600
- cache_values: bfloat16 [2, 512, 1024, 512], P('guide', ('batch', 'tensor')), may hold values from -6 to 6
- cache_len: int32 [2, 512], P('guide', ('batch', 'tensor')), may hold values from 1 to 1024, as said below
- w_out: bfloat16 [2048, 2048], P('tensor'), may hold values from -0.125 to 0.125
- mlp_gain: float32 [2048], replicated, may hold values from 0.25 to 1.75
- w_gate: bfloat16 [2048, 8192], P(None, 'tensor'), may hold values from -0.125 to 0.125
- w_up: bfloat16 [2048, 8192], P(None, 'tensor'), may hold values from -0.125 to 0.125
- w_down: bfloat16 [8192, 2048], P('tensor'), may hold values from -0.0625 to 0.0625
- final_gain: float32 [2048], replicated, may hold values from 0.25 to 1.75
- lm_head: bfloat16 [65536, 2048], P(('guide', 'tensor')), may hold values from -128 to 128
- next_gain: float32 [2048], replicated, may hold values from 0.25 to 1.75
- w_next: bfloat16 [2048, 3072], P(None, 'tensor'), may hold values from -0.125 to 0.125
- tenant_counts: int32 [4], replicated, may hold values from 1 to 256, 512 in all
- guide_level: int32 [4], replicated, may hold values from 4 to 16
Outputs:
- logprobs: float32 [512, 65536], P('batch', ('guide', 'tensor'))
- layer_out: bfloat16 [2, 512, 2048], P('guide', ('batch', 'tensor'))
- next_qkv: bfloat16 [2, 512, 3072], P('guide', 'batch', 'tensor')
Inputs may be any that keep to these rules, and one draw needn't show every extreme that they name: `cache_len`: in each branch some request has 1024 cached tokens.
All inputs are finite; a program needn't handle non-finite values.
Results may differ from a plain program's by a relative error of at most 0.024.
Values may be sent and summed in bfloat16 or wider, within the bound.
A program may use at most 128 MiB of HBM per device.

v0:
```python
import math
import jax
import jax.numpy as jnp
from jax import lax
from jax.sharding import PartitionSpec as P

D = 2048
HEADS = 32
KV_HEADS = 8
HEAD_DIM = 64
TENANTS = 4
EPSILON = 1e-05
ROPE_BASE = 500000.0
MASKED = -1e30


def from_partner(block, axis, bit):
    count = lax.axis_size(axis)
    route = []
    for low in range(count):
        high = low | 1 << bit
        if high != low and high < count:
            route += [(low, high), (high, low)]
    return lax.ppermute(block, axis, route)


def rms_norm(values, gain):
    widened = values.astype(jnp.float32)
    factor = lax.rsqrt(jnp.mean(widened * widened, axis=-1, keepdims=True) + EPSILON)
    return (widened * factor * gain).astype(jnp.bfloat16)


def scaled_freq(head_size):
    half_dim = head_size // 2
    steps_up = jnp.arange(half_dim, dtype=jnp.float32)
    base_freq = jnp.exp(steps_up * (-2.0 * math.log(ROPE_BASE) / head_size))
    wavelen = 2.0 * math.pi / base_freq
    smooth = (8192.0 / wavelen - 1.0) / 3.0
    middle = (1.0 - smooth) * base_freq / 32.0 + smooth * base_freq
    return jnp.where(
        wavelen < 2048.0, base_freq, jnp.where(wavelen > 8192.0, base_freq / 32.0, middle)
    )


def rotate(values, position):
    half_dim = values.shape[-1] // 2
    freq = scaled_freq(values.shape[-1])
    angle = position * freq
    cosine = jnp.cos(angle)
    sine = jnp.sin(angle)
    first = values[..., :half_dim].astype(jnp.float32)
    second = values[..., half_dim:].astype(jnp.float32)
    joined = jnp.concatenate(
        [first * cosine - second * sine, second * cosine + first * sine], axis=-1
    )
    return joined.astype(jnp.bfloat16)


def swiglu(normed, w_gate, w_up):
    gate = jnp.dot(normed, w_gate, preferred_element_type=jnp.float32)
    upward = jnp.dot(normed, w_up, preferred_element_type=jnp.float32)
    return (jax.nn.silu(gate) * upward).astype(jnp.bfloat16)


def attend(request_side, keys, values, lengths):
    count = request_side.shape[0]
    kv_width = KV_HEADS * HEAD_DIM
    per_group = HEADS // KV_HEADS
    scale = HEAD_DIM ** (-0.5)
    slot_count = keys.shape[1]
    position = lengths.astype(jnp.float32)[:, None, None]
    queries = rotate(request_side[:, :D].reshape(count, HEADS, HEAD_DIM), position)
    queries = queries.reshape(count, KV_HEADS, per_group, HEAD_DIM)
    new_keys = rotate(
        request_side[:, D : D + kv_width].reshape(count, KV_HEADS, HEAD_DIM), position
    )
    new_values = request_side[:, D + kv_width :].reshape(count, KV_HEADS, HEAD_DIM)
    keys_split = keys.reshape(count, slot_count, KV_HEADS, HEAD_DIM)
    values_split = values.reshape(count, slot_count, KV_HEADS, HEAD_DIM)
    fresh = (
        jnp.einsum("rkgd,rkd->rkg", queries, new_keys, preferred_element_type=jnp.float32) * scale
    )
    slots = jnp.arange(slot_count, dtype=jnp.int32)
    live_mask = (slots[None, :] < lengths[:, None])[:, None, None, :]
    scores = (
        jnp.einsum("rkgd,rlkd->rkgl", queries, keys_split, preferred_element_type=jnp.float32)
        * scale
    )
    scores = jnp.where(live_mask, scores, MASKED)
    peak = jnp.maximum(jnp.max(scores, axis=-1), fresh)
    expd = jnp.where(live_mask, jnp.exp(scores - peak[..., None]), 0.0)
    total = jnp.sum(expd, axis=-1)
    weighted = jnp.einsum(
        "rkgl,rlkd->rkgd",
        expd.astype(jnp.bfloat16),
        values_split,
        preferred_element_type=jnp.float32,
    )
    fresh_exp = jnp.exp(fresh - peak)
    total = total + fresh_exp
    fresh_prob = fresh_exp.astype(jnp.bfloat16).astype(jnp.float32)
    weighted = weighted + fresh_prob[..., None] * new_values.astype(jnp.float32)[:, :, None, :]
    return (weighted / total[..., None]).reshape(count, D).astype(jnp.bfloat16)


def local(
    stream,
    attn_gain,
    w_qkv,
    cache_keys,
    cache_values,
    cache_len,
    w_out,
    mlp_gain,
    w_gate,
    w_up,
    w_down,
    final_gain,
    lm_head,
    next_gain,
    w_next,
    tenant_counts,
    guide_level,
):
    own_rows = stream[0]
    projected = jnp.dot(
        lax.all_gather(rms_norm(own_rows, attn_gain), "tensor", axis=0, tiled=True),
        w_qkv,
        preferred_element_type=jnp.float32,
    ).astype(jnp.bfloat16)
    request_side = lax.all_to_all(projected, "tensor", split_axis=0, concat_axis=1, tiled=True)
    mixed = attend(request_side, cache_keys[0], cache_values[0], cache_len[0])
    head_side = lax.all_to_all(mixed, "tensor", split_axis=1, concat_axis=0, tiled=True)
    selected = head_side
    attn_share = lax.psum_scatter(
        jnp.dot(selected, w_out, preferred_element_type=jnp.float32).astype(jnp.bfloat16),
        "tensor",
        scatter_dimension=0,
        tiled=True,
    ).astype(jnp.float32)
    after_attn = (own_rows.astype(jnp.float32) + attn_share).astype(jnp.bfloat16)
    hidden = swiglu(
        lax.all_gather(rms_norm(after_attn, mlp_gain), "tensor", axis=0, tiled=True), w_gate, w_up
    )
    selected = hidden
    mlp_share = lax.psum_scatter(
        jnp.dot(selected, w_down, preferred_element_type=jnp.float32).astype(jnp.bfloat16),
        "tensor",
        scatter_dimension=0,
        tiled=True,
    ).astype(jnp.float32)
    layer_rows = (after_attn.astype(jnp.float32) + mlp_share).astype(jnp.bfloat16)
    all_out = lax.all_gather(layer_rows, "tensor", axis=0, tiled=True)
    next_rows = jnp.dot(
        rms_norm(all_out, next_gain), w_next, preferred_element_type=jnp.float32
    ).astype(jnp.bfloat16)
    final = rms_norm(all_out, final_gain)
    partner = from_partner(final, "guide", 0)
    is_cond = lax.axis_index("guide") == 0
    cond_rows = jnp.where(is_cond, final, partner)
    uncond_rows = jnp.where(is_cond, partner, final)
    batch_rows = final.shape[0]
    logits = lax.dot_general(
        jnp.concatenate([cond_rows, uncond_rows], axis=0),
        lm_head,
        (((1,), (1,)), ((), ())),
        preferred_element_type=jnp.float32,
    )
    cond_logits = logits[:batch_rows]
    uncond_logits = logits[batch_rows:]
    bounds = jnp.cumsum(tenant_counts)[:-1]
    request_ids = lax.axis_index("batch") * batch_rows + jnp.arange(batch_rows, dtype=jnp.int32)
    tenant = jnp.sum((request_ids[:, None] >= bounds[None, :]).astype(jnp.int32), axis=1)
    chosen = (tenant[:, None] == jnp.arange(TENANTS, dtype=jnp.int32)[None, :]).astype(jnp.float32)
    weight = jnp.sum(chosen * guide_level.astype(jnp.float32)[None, :], axis=1) * 0.25
    guided = uncond_logits + weight[:, None] * (cond_logits - uncond_logits)
    peak = lax.pmax(jnp.max(guided, axis=1), ("guide", "tensor"))
    mass = lax.psum(jnp.sum(jnp.exp(guided - peak[:, None]), axis=1), ("guide", "tensor"))
    logprobs = guided - peak[:, None] - jnp.log(mass)[:, None]
    return (logprobs, layer_rows[None], next_rows[None])


def solution(mesh):
    in_specs = (
        P("guide", ("batch", "tensor"), None),
        P(),
        P(None, "tensor"),
        P("guide", ("batch", "tensor"), None, None),
        P("guide", ("batch", "tensor"), None, None),
        P("guide", ("batch", "tensor")),
        P("tensor", None),
        P(),
        P(None, "tensor"),
        P(None, "tensor"),
        P("tensor", None),
        P(),
        P(("guide", "tensor"), None),
        P(),
        P(None, "tensor"),
        P(),
        P(),
    )
    out_specs = (
        P("batch", ("guide", "tensor")),
        P("guide", ("batch", "tensor"), None),
        P("guide", "batch", "tensor"),
    )
    return jax.shard_map(local, mesh=mesh, in_specs=in_specs, out_specs=out_specs, check_vma=False)
```

profile of v0, /device:TPU:1, one launch (start us, length us, event | category | flops | bytes accessed | tf_op | source)
XLA Modules:
  0.0 462.2 jit_solution(6862168536438569131)
XLA Ops:
  7.2 0.0 copy-start
  7.2 0.0 copy-start.5
  7.2 1.0 fusion.39
  8.2 0.8 fusion.41
  9.1 20.0 %all_gather.9 = bf16[128,2048]{1,0:T(8,128)(2,1)S(1)} all-gather(bf16[8,2048]{1,0:T(8,128)(2,1)S(1)} %fusion.41), channel_id=1, replica_groups=mesh['guide'=2,'tensor'=16,'batch'=4] {'tensor'}, dimensions={0}, use_global_device_ids=true | all-gather | bytes 557056 | tf_op jit(solution)/shard_map/all_gather | solution.py:127
  29.0 1.5 convolution_convert_fusion.3
  30.5 0.7 copy.32
  31.3 4.7 %all-to-all-start = ((bf16[16,8,192]{2,1,0:T(8,128)(2,1)}), bf16[16,8,192]{2,1,0:T(8,128)(2,1)S(1)}, u32[]{:S(2)}, u32[]{:S(2)}) async-start(bf16[16,8,192]{2,1,0:T(8,128)(2,1)} %bitcast.3), calls=%async_computation | async-start | bytes 131072 | tf_op jit(solution)/shard_map/all_to_all | solution.py:131
  36.0 0.0 all-reduce.5.cloned.1.call-start
  36.0 0.0 copy-done.5
  36.1 0.1 multiply_cosine_fusion
  36.2 0.1 iota_compare_fusion
  36.3 11.4 %copy.34 = bf16[1,8,1024,512]{2,3,1,0:T(8,128)(2,1)} copy(bf16[1,8,1024,512]{3,2,1,0:T(8,128)(2,1)} %param.20) | data formatting | bytes 16777216 | tf_op args[3]
  47.7 11.5 %copy.35 = bf16[1,8,1024,512]{2,3,1,0:T(8,128)(2,1)} copy(bf16[1,8,1024,512]{3,2,1,0:T(8,128)(2,1)} %param.21) | data formatting | bytes 16777216 | tf_op args[4]
  59.1 0.0 all-to-all-done
  59.2 0.1 all_to_all.29
  59.3 0.1 reshape.189
  59.4 0.1 reshape.188
  59.5 0.1 fusion.44
  59.6 0.1 fusion.31
  59.7 0.1 maximum_bitcast_fusion
  59.8 0.3 fusion.48
  60.1 4.8 %fusion.57 = (f32[8,8,4]{2,1,0:T(8,128)S(1)}, f32[8,8,4,1024]{3,2,1,0:T(4,128)S(1)}) fusion(bf16[8,1024,8,64]{1,3,2,0:T(8,128)(2,1)} %bitcast.42, bf16[8,8,4,32]{3,2,1,0:T(4,128)(2,1)S(1)} %bitcast.47, bf16[8,8,4,32]{3,2,1,0:T(4,128)(2,1)S(1)} %bitcast.45, pred[8,1024]{1,0:T(8,128)(4,1)S(1)} %iota_compare_fusion), kind=kOutput, calls=%fused_computation.103 | convolution fusion | flops 34406144 | bytes 9479168 | tf_op jit(solution)/shard_map/rkgd,rlkd->rkgl/dot_general | solution.py:86
  64.8 0.6 fusion.16
  65.5 0.1 reshape.192
  65.6 5.8 %fusion.5 = bf16[8,8,4,64]{3,2,1,0:T(4,128)(2,1)S(1)} fusion(bf16[8,1024,8,64]{1,3,2,0:T(8,128)(2,1)} %bitcast.43, f32[8,8,4,1024]{3,2,1,0:T(4,128)S(1)} %get-tuple-element.20, f32[8,8,4]{2,1,0:T(8,128)S(1)} %multiply_maximum_fusion, pred[8,1024]{1,0:T(8,128)(4,1)S(1)} %iota_compare_fusion, f32[8,8,4]{2,1,0:T(8,128)S(1)} %get-tuple-element.12, ...), kind=kOutput, calls=%fused_computation.12 | convolution fusion | flops 34406400 | bytes 9497600 | tf_op jit(solution)/shard_map/rkgl,rlkd->rkgd/dot_general | solution.py:93
  71.3 0.1 convert_element_type.124
  71.5 12.9 %all_to_all.35 = bf16[8,16,128]{2,0,1:T(8,128)(2,1)S(1)} all-to-all(bf16[8,16,128]{2,0,1:T(8,128)(2,1)S(1)} %copy.36), channel_id=1, replica_groups=mesh['guide'=2,'tensor'=16,'batch'=4] {'tensor'}, dimensions={1} | all-to-all | bytes 65536 | tf_op jit(solution)/shard_map/all_to_all | solution.py:133
  84.4 2.1 convolution_convert_fusion.1
  86.5 0.0 all-reduce.5.cloned.1.call-update
  86.5 0.0 all-reduce.7.cloned.1.call-start
  86.6 0.0 copy-done.9
  86.6 0.6 dynamic-slice
  87.8 88.3 %all-reduce.5.cloned.1.call-done = bf16[128,2048]{1,0:T(8,128)(2,1)} async-done(((bf16[128,2048]{1,0:T(8,128)(2,1)}), bf16[128,2048]{1,0:T(8,128)(2,1)}) %all-reduce.5.cloned.1.call-update) | async-done | bytes 524304
  176.1 0.0 copy-done.1
  176.1 0.9 fusion.35
  177.0 0.0 copy-done.4
  177.0 0.1 fusion.37
  177.1 17.4 %all_gather.10 = bf16[128,2048]{1,0:T(8,128)(2,1)S(1)} all-gather(bf16[8,2048]{1,0:T(8,128)(2,1)S(1)} %fusion.37), channel_id=1, replica_groups=mesh['guide'=2,'tensor'=16,'batch'=4] {'tensor'}, dimensions={0}, use_global_device_ids=true | all-gather | bytes 557056 | tf_op jit(solution)/shard_map/all_gather | solution.py:143
  194.5 2.0 fusion.58
  196.6 0.0 copy-done
  196.6 0.0 copy-start.7
  196.6 0.0 copy-start.3
  196.6 3.2 convolution_convert_fusion
  199.8 0.0 all-reduce.7.cloned.1.call-update
  199.9 0.2 reduce-window.4
  200.1 0.1 convert_reduce_fusion
  200.2 89.2 %all-reduce.7.cloned.1.call-done = bf16[128,2048]{1,0:T(8,128)(2,1)} async-done(((bf16[128,2048]{1,0:T(8,128)(2,1)}), bf16[128,2048]{1,0:T(8,128)(2,1)}) %all-reduce.7.cloned.1.call-update) | async-done | bytes 524304
  289.3 0.8 fusion.38
  290.1 0.0 copy-start.2
  290.1 17.4 %all_gather.11 = bf16[128,2048]{1,0:T(8,128)(2,1)S(1)} all-gather(bf16[8,2048]{1,0:T(8,128)(2,1)S(1)} %fusion.38), channel_id=1, replica_groups=mesh['guide'=2,'tensor'=16,'batch'=4] {'tensor'}, dimensions={0}, use_global_device_ids=true | all-gather | bytes 557056 | tf_op jit(solution)/shard_map/all_gather | solution.py:153
  307.5 0.2 fusion.9
  307.7 0.2 fusion.7
  307.9 8.1 %collective-permute-start = (bf16[128,2048]{1,0:T(8,128)(2,1)S(1)}, bf16[128,2048]{1,0:T(8,128)(2,1)}, u32[]{:S(2)}, u32[]{:S(2)}) collective-permute-start(bf16[128,2048]{1,0:T(8,128)(2,1)S(1)} %fusion.7), channel_id=1, source_target_pairs={{0,64},{64,0},{1,65},{65,1},{2,66},{66,2},{3,67},{67,3},{4,68},{68... | collective-permute-start | bytes 1572872 | tf_op jit(solution)/shard_map/ppermute | solution.py:24
  316.1 0.1 select_reduce_fusion
  316.1 2.2 fusion.6
  318.4 0.0 collective-permute-done
  318.4 1.4 broadcast_select_fusion.1
  319.8 5.7 %fusion.12 = f32[256,2048]{1,0:T(8,128)S(1)} fusion(bf16[2048,2048]{1,0:T(8,128)(2,1)} %param.29, bf16[128,2048]{1,0:T(8,128)(2,1)S(1)} %get-tuple-element.8, bf16[128,2048]{1,0:T(8,128)(2,1)S(1)} %get-tuple-element.7), kind=kOutput, calls=%fused_computation.22 | convolution fusion | flops 2149580800 | bytes 11534336 | tf_op jit(solution)/shard_map/dot_general | solution.py:163
  325.5 0.4 fusion.54
  326.0 65.0 %pmax.7 = f32[128]{0:T(128)S(1)} all-reduce(f32[128]{0:T(128)S(1)} %get-tuple-element.3), channel_id=1, replica_groups=mesh['guide'=2,'tensor'=16,'batch'=4] {'guide','tensor'}, use_global_device_ids=true, to_apply=%region_11.12 | all-reduce | flops 128 | bytes 1024 | tf_op jit(solution)/shard_map/pmax | solution.py:177
  391.0 0.3 exponential_reduce_fusion
  391.3 62.9 %psum.7 = f32[128]{0:T(128)S(1)} all-reduce(f32[128]{0:T(128)S(1)} %exponential_reduce_fusion), channel_id=1, replica_groups=mesh['guide'=2,'tensor'=16,'batch'=4] {'guide','tensor'}, use_global_device_ids=true, to_apply=%region_13.14 | all-reduce | flops 128 | bytes 1024 | tf_op jit(solution)/shard_map/psum | solution.py:178
  454.2 1.1 subtract_subtract_fusion
  (26 shorter events, 0.1 us)
Async XLA Ops:
  7.2 189.4 %copy-start = (bf16[512,2048]{1,0:T(8,128)(2,1)S(1)}, bf16[512,2048]{1,0:T(8,128)(2,1)}, u32[]{:S(2)}) copy-start(bf16[512,2048]{1,0:T(8,128)(2,1)} %param.27) | copy-start | bytes 6291460
  7.2 28.9 %copy-start.5 = (s32[1,8]{1,0:T(1,128)S(1)}, s32[1,8]{1,0:T(1,128)}, u32[]{:S(2)}) copy-start(s32[1,8]{1,0:T(1,128)} %param.22) | copy-start | bytes 100
  31.3 27.9 %all-to-all-start = ((bf16[16,8,192]{2,1,0:T(8,128)(2,1)}), bf16[16,8,192]{2,1,0:T(8,128)(2,1)S(1)}, u32[]{:S(2)}, u32[]{:S(2)}) async-start(bf16[16,8,192]{2,1,0:T(8,128)(2,1)} %bitcast.3), calls=%async_computation | async-start | bytes 131072 | tf_op jit(solution)/shard_map/all_to_all | solution.py:131
  36.0 140.2 %all-reduce.5.cloned.1.call-start = ((), (), s32[]{:S(2)}) async-start(), calls=%async_computation.2 | async-start | bytes 1048576
  65.5 21.1 %copy-start.9 = (u32[128]{0:T(128)S(1)}, u32[128]{0:T(128)}, u32[]{:S(2)}) copy-start(u32[128]{0:T(128)} %constant.67) | copy-start | bytes 1540
  65.5 110.6 %copy-start.1 = (bf16[1,8,2048]{2,1,0:T(8,128)(2,1)S(1)}, bf16[1,8,2048]{2,1,0:T(8,128)(2,1)}, u32[]{:S(2)}) copy-start(bf16[1,8,2048]{2,1,0:T(8,128)(2,1)} %param.17) | copy-start | bytes 98308
  65.6 111.5 %copy-start.4 = (f32[2048]{0:T(1024)S(1)}, f32[2048]{0:T(1024)}, u32[]{:S(2)}) copy-start(f32[2048]{0:T(1024)} %param.24) | copy-start | bytes 24580
  86.5 202.8 %all-reduce.7.cloned.1.call-start = ((), (), s32[]{:S(2)}) async-start(), calls=%async_computation.3 | async-start | bytes 1048576
  196.6 3.3 copy-start.7
  196.6 111.1 %copy-start.3 = (f32[2048]{0:T(1024)S(1)}, f32[2048]{0:T(1024)}, u32[]{:S(2)}) copy-start(f32[2048]{0:T(1024)} %param.28) | copy-start | bytes 24580
  199.8 116.2 %copy-start.8 = (s32[4]{0:T(128)S(1)}, s32[4]{0:T(128)}, u32[]{:S(2)}) copy-start(s32[4]{0:T(128)} %param.33) | copy-start | bytes 52
  199.8 116.3 %copy-start.6 = (f32[2048]{0:T(1024)S(1)}, f32[2048]{0:T(1024)}, u32[]{:S(2)}) copy-start(f32[2048]{0:T(1024)} %param.30) | copy-start | bytes 24580
  290.1 29.7 %copy-start.2 = (bf16[8,2048]{1,0:T(8,128)(2,1)}, bf16[8,2048]{1,0:T(8,128)(2,1)S(1)}, u32[]{:S(2)}) copy-start(bf16[8,2048]{1,0:T(8,128)(2,1)S(1)} %fusion.38) | copy-start | bytes 98308
  307.9 10.4 %collective-permute-start = (bf16[128,2048]{1,0:T(8,128)(2,1)S(1)}, bf16[128,2048]{1,0:T(8,128)(2,1)}, u32[]{:S(2)}, u32[]{:S(2)}) collective-permute-start(bf16[128,2048]{1,0:T(8,128)(2,1)S(1)} %fusion.7), channel_id=1, source_target_pairs={{0,64},{64,0},{1,65},{65,1},{2,66},{66,2},{3,67},{67,3},{4,68},{68... | collective-permute-start | bytes 1572872 | tf_op jit(solution)/shard_map/ppermute | solution.py:24
Sparse Core Ops, SparseCore 0:
  86.7 89.4 all-reduce.4
  200.0 89.2 all-reduce.6
where the time goes:
time: 464 us; the launch traced here: 462 us
  blocking collectives  196 us (42%)
  waiting for transfers between devices  178 us (38%)
  matrix products  27.7 us (6%)
  local copies, waits for them, and re-layouts  24.8 us (5%)
  between operations  14.9 us (3%)
  starting transfers between devices  12.9 us (3%)
  other arithmetic  8.77 us (2%)
    unnamed x4, waiting for transfers between devices  177 us
    pmax x1, blocking collectives, local(): peak = lax.pmax(jnp.max(guided, axis=1), ('guide', 'tensor'))  65 us
    psum x1, blocking collectives, local(): lax.psum(jnp.sum(jnp.exp(guided - peak[:, None]), axis=1), ('guide', 'ten...  62.9 us
    unnamed x23, local copies, waits for them, and re-layouts  23.5 us
    all_gather x1, blocking collectives, local(): lax.all_gather(rms_norm(own_rows, attn_gain), 'tensor', axis=0, tiled=True)  20 us
    all_gather x1, blocking collectives, local(): all_out = lax.all_gather(layer_rows, 'tensor', axis=0, tiled=True)  17.4 us
    all_gather x1, blocking collectives, local(): lax.all_gather(rms_norm(after_attn, mlp_gain), 'tensor', axis=0, tiled=True)  17.4 us
    all_to_all x1, blocking collectives, local(): lax.all_to_all(mixed, 'tensor', split_axis=1, concat_axis=0, tiled=True)  12.9 us
  transfers between devices with their start and end apart: 4, of which 2 were waited for; matrix products, arithmetic and copies ran while one was open for 6% of the time, Pallas kernels for 0%

commit v1 on v0

--- a/solution.py
+++ b/solution.py
@@ -150,7 +150,14 @@
         tiled=True,
     ).astype(jnp.float32)
     layer_rows = (after_attn.astype(jnp.float32) + mlp_share).astype(jnp.bfloat16)
-    all_out = lax.all_gather(layer_rows, "tensor", axis=0, tiled=True)
+    ring = [layer_rows]
+    for hop in range(15):
+        ring.append(lax.ppermute(ring[-1], "tensor", [(dev, (dev + 1) % 16) for dev in range(16)]))
+    all_out = jnp.roll(
+        jnp.concatenate(ring[::-1], axis=0),
+        (lax.axis_index("tensor") + 1) * ring[0].shape[0],
+        axis=0,
+    )
     next_rows = jnp.dot(
         rms_norm(all_out, next_gain), w_next, preferred_element_type=jnp.float32
     ).astype(jnp.bfloat16)

time: 464 us -> 558 us (1.20)
  waiting for transfers between devices: 178 us -> 268 us
  blocking collectives: 196 us -> 178 us
  starting transfers between devices: 12.9 us -> 24.3 us
  local copies, waits for them, and re-layouts: 24.8 us -> 31.7 us
    ppermute x0 -> x15, waiting for transfers between devices: none -> 90.1 us  [local(): lax.ppermute(ring[-1], 'tensor', [(dev, (dev + 1) % 16) for dev in range(...]
    all_gather x1 -> x0, blocking collectives: 17.4 us -> none  [local(): all_out = lax.all_gather(layer_rows, 'tensor', axis=0, tiled=True)]
    ppermute x1, starting transfers between devices: 8.1 us -> 19.1 us  [from_partner(): return lax.ppermute(block, axis, route)]
    unnamed x23 -> x62, local copies, waits for them, and re-layouts: 23.5 us -> 29.8 us
  transfers between devices with their start and end apart: 4 -> 19, of which waited for: 2 -> 17; matrix products, arithmetic and copies ran while one was open for 6% -> 5% of each run, Pallas kernels for 0% -> 0%
where the time goes in v1:
time: 558 us; the launch traced here: 556 us
  waiting for transfers between devices  268 us (48%)
  blocking collectives  178 us (32%)
  local copies, waits for them, and re-layouts  31.7 us (6%)
  matrix products  27.7 us (5%)
  starting transfers between devices  24.3 us (4%)
  between operations  15.1 us (3%)
  other arithmetic  10.7 us (2%)
    unnamed x4, waiting for transfers between devices  178 us
    ppermute x15, waiting for transfers between devices, local(): lax.ppermute(ring[-1], 'tensor', [(dev, (dev + 1) % 16) for dev in range(...  90.1 us
    psum x1, blocking collectives, local(): lax.psum(jnp.sum(jnp.exp(guided - peak[:, None]), axis=1), ('guide', 'ten...  65.3 us
    pmax x1, blocking collectives, local(): peak = lax.pmax(jnp.max(guided, axis=1), ('guide', 'tensor'))  62.7 us
    unnamed x62, local copies, waits for them, and re-layouts  29.8 us
    all_gather x1, blocking collectives, local(): lax.all_gather(rms_norm(own_rows, attn_gain), 'tensor', axis=0, tiled=True)  20 us
    ppermute x1, starting transfers between devices, from_partner(): return lax.ppermute(block, axis, route)  19.1 us
    all_gather x1, blocking collectives, local(): lax.all_gather(rms_norm(after_attn, mlp_gain), 'tensor', axis=0, tiled=True)  17.4 us
  transfers between devices with their start and end apart: 19, of which 17 were waited for; matrix products, arithmetic and copies ran while one was open for 5% of the time, Pallas kernels for 0%

profile of v1, /device:TPU:1, one launch (start us, length us, event | category | flops | bytes accessed | tf_op | source)
XLA Modules:
  0.0 555.7 jit_solution(3041852898659732973)
XLA Ops:
  7.2 1.0 fusion.40
  8.2 0.8 fusion.42
  9.1 20.0 %all_gather.6 = bf16[128,2048]{1,0:T(8,128)(2,1)S(1)} all-gather(bf16[8,2048]{1,0:T(8,128)(2,1)S(1)} %fusion.42), channel_id=1, replica_groups=mesh['guide'=2,'tensor'=16,'batch'=4] {'tensor'}, dimensions={0}, use_global_device_ids=true | all-gather | bytes 557056 | tf_op jit(solution)/shard_map/all_gather | solution.py:127
  29.0 1.5 convolution_convert_fusion.3
  30.5 0.7 copy.32
  31.3 4.7 all-to-all-start
  36.3 11.4 %copy.34 = bf16[1,8,1024,512]{2,3,1,0:T(8,128)(2,1)} copy(bf16[1,8,1024,512]{3,2,1,0:T(8,128)(2,1)} %param.20) | data formatting | bytes 16777216 | tf_op args[3]
  47.7 11.5 %copy.35 = bf16[1,8,1024,512]{2,3,1,0:T(8,128)(2,1)} copy(bf16[1,8,1024,512]{3,2,1,0:T(8,128)(2,1)} %param.21) | data formatting | bytes 16777216 | tf_op args[4]
  59.2 0.1 all_to_all.29
  59.4 0.1 reshape.188
  59.8 0.3 fusion.49
  60.1 4.8 fusion.59
  64.8 0.6 fusion.16
  65.5 5.8 %fusion.5 = bf16[8,8,4,64]{3,2,1,0:T(4,128)(2,1)S(1)} fusion(bf16[8,1024,8,64]{1,3,2,0:T(8,128)(2,1)} %bitcast.43, f32[8,8,4,1024]{3,2,1,0:T(4,128)S(1)} %get-tuple-element.20, f32[8,8,4]{2,1,0:T(8,128)S(1)} %multiply_maximum_fusion, pred[8,1024]{1,0:T(8,128)(4,1)S(1)} %iota_compare_fusion, f32[8,8,4]{2,1,0:T(8,128)S(1)} %get-tuple-element.12, ...), kind=kOutput, calls=%fused_computation.12 | convolution fusion | flops 34406400 | bytes 9497600 | tf_op jit(solution)/shard_map/rkgl,rlkd->rkgd/dot_general | solution.py:93
  71.3 0.1 convert_element_type.124
  71.5 12.9 %all_to_all.35 = bf16[8,16,128]{2,0,1:T(8,128)(2,1)S(1)} all-to-all(bf16[8,16,128]{2,0,1:T(8,128)(2,1)S(1)} %copy.36), channel_id=1, replica_groups=mesh['guide'=2,'tensor'=16,'batch'=4] {'tensor'}, dimensions={1} | all-to-all | bytes 65536 | tf_op jit(solution)/shard_map/all_to_all | solution.py:133
  84.4 2.1 convolution_convert_fusion.1
  86.6 0.6 dynamic-slice
  87.8 88.3 %all-reduce.5.cloned.1.call-done = bf16[128,2048]{1,0:T(8,128)(2,1)} async-done(((bf16[128,2048]{1,0:T(8,128)(2,1)}), bf16[128,2048]{1,0:T(8,128)(2,1)}) %all-reduce.5.cloned.1.call-update) | async-done | bytes 524304
  176.1 0.9 fusion.36
  177.1 17.4 %all_gather.7 = bf16[128,2048]{1,0:T(8,128)(2,1)S(1)} all-gather(bf16[8,2048]{1,0:T(8,128)(2,1)S(1)} %fusion.38), channel_id=1, replica_groups=mesh['guide'=2,'tensor'=16,'batch'=4] {'tensor'}, dimensions={0}, use_global_device_ids=true | all-gather | bytes 557056 | tf_op jit(solution)/shard_map/all_gather | solution.py:143
  194.5 2.0 fusion.60
  196.6 3.2 convolution_convert_fusion
  199.8 89.6 %all-reduce.7.cloned.1.call-done = bf16[128,2048]{1,0:T(8,128)(2,1)} async-done(((bf16[128,2048]{1,0:T(8,128)(2,1)}), bf16[128,2048]{1,0:T(8,128)(2,1)}) %all-reduce.7.cloned.1.call-update) | async-done | bytes 524304
  289.4 0.8 fusion.39
  290.2 0.3 collective-permute-start
  290.5 5.8 %collective-permute-done = bf16[8,2048]{1,0:T(8,128)(2,1)S(1)} collective-permute-done((bf16[8,2048]{1,0:T(8,128)(2,1)S(1)}, bf16[8,2048]{1,0:T(8,128)(2,1)S(1)}, u32[]{:S(2)}, u32[]{:S(2)}) %collective-permute-start) | collective-permute-done | bytes 32800 | tf_op jit(solution)/shard_map/ppermute | solution.py:155
  296.4 6.1 %collective-permute-done.1 = bf16[8,2048]{1,0:T(8,128)(2,1)S(1)} collective-permute-done((bf16[8,2048]{1,0:T(8,128)(2,1)S(1)}, bf16[8,2048]{1,0:T(8,128)(2,1)S(1)}, u32[]{:S(2)}, u32[]{:S(2)}) %collective-permute-start.1) | collective-permute-done | bytes 32800 | tf_op jit(solution)/shard_map/ppermute | solution.py:155
  302.4 6.1 %collective-permute-done.2 = bf16[8,2048]{1,0:T(8,128)(2,1)S(1)} collective-permute-done((bf16[8,2048]{1,0:T(8,128)(2,1)S(1)}, bf16[8,2048]{1,0:T(8,128)(2,1)S(1)}, u32[]{:S(2)}, u32[]{:S(2)}) %collective-permute-start.2) | collective-permute-done | bytes 32800 | tf_op jit(solution)/shard_map/ppermute | solution.py:155
  308.5 6.1 %collective-permute-done.3 = bf16[8,2048]{1,0:T(8,128)(2,1)S(1)} collective-permute-done((bf16[8,2048]{1,0:T(8,128)(2,1)S(1)}, bf16[8,2048]{1,0:T(8,128)(2,1)S(1)}, u32[]{:S(2)}, u32[]{:S(2)}) %collective-permute-start.3) | collective-permute-done | bytes 32800 | tf_op jit(solution)/shard_map/ppermute | solution.py:155
  314.6 6.5 %collective-permute-done.4 = bf16[8,2048]{1,0:T(8,128)(2,1)S(1)} collective-permute-done((bf16[8,2048]{1,0:T(8,128)(2,1)S(1)}, bf16[8,2048]{1,0:T(8,128)(2,1)S(1)}, u32[]{:S(2)}, u32[]{:S(2)}) %collective-permute-start.4) | collective-permute-done | bytes 32800 | tf_op jit(solution)/shard_map/ppermute | solution.py:155
  321.1 6.1 %collective-permute-done.5 = bf16[8,2048]{1,0:T(8,128)(2,1)S(1)} collective-permute-done((bf16[8,2048]{1,0:T(8,128)(2,1)S(1)}, bf16[8,2048]{1,0:T(8,128)(2,1)S(1)}, u32[]{:S(2)}, u32[]{:S(2)}) %collective-permute-start.5) | collective-permute-done | bytes 32800 | tf_op jit(solution)/shard_map/ppermute | solution.py:155
  327.2 6.1 %collective-permute-done.6 = bf16[8,2048]{1,0:T(8,128)(2,1)S(1)} collective-permute-done((bf16[8,2048]{1,0:T(8,128)(2,1)S(1)}, bf16[8,2048]{1,0:T(8,128)(2,1)S(1)}, u32[]{:S(2)}, u32[]{:S(2)}) %collective-permute-start.6) | collective-permute-done | bytes 32800 | tf_op jit(solution)/shard_map/ppermute | solution.py:155
  333.3 6.1 %collective-permute-done.7 = bf16[8,2048]{1,0:T(8,128)(2,1)S(1)} collective-permute-done((bf16[8,2048]{1,0:T(8,128)(2,1)S(1)}, bf16[8,2048]{1,0:T(8,128)(2,1)S(1)}, u32[]{:S(2)}, u32[]{:S(2)}) %collective-permute-start.7) | collective-permute-done | bytes 32800 | tf_op jit(solution)/shard_map/ppermute | solution.py:155
  339.4 6.1 %collective-permute-done.8 = bf16[8,2048]{1,0:T(8,128)(2,1)S(1)} collective-permute-done((bf16[8,2048]{1,0:T(8,128)(2,1)S(1)}, bf16[8,2048]{1,0:T(8,128)(2,1)S(1)}, u32[]{:S(2)}, u32[]{:S(2)}) %collective-permute-start.8) | collective-permute-done | bytes 32800 | tf_op jit(solution)/shard_map/ppermute | solution.py:155
  345.4 6.1 %collective-permute-done.9 = bf16[8,2048]{1,0:T(8,128)(2,1)S(1)} collective-permute-done((bf16[8,2048]{1,0:T(8,128)(2,1)S(1)}, bf16[8,2048]{1,0:T(8,128)(2,1)S(1)}, u32[]{:S(2)}, u32[]{:S(2)}) %collective-permute-start.9) | collective-permute-done | bytes 32800 | tf_op jit(solution)/shard_map/ppermute | solution.py:155
  351.5 6.1 %collective-permute-done.10 = bf16[8,2048]{1,0:T(8,128)(2,1)S(1)} collective-permute-done((bf16[8,2048]{1,0:T(8,128)(2,1)S(1)}, bf16[8,2048]{1,0:T(8,128)(2,1)S(1)}, u32[]{:S(2)}, u32[]{:S(2)}) %collective-permute-start.10) | collective-permute-done | bytes 32800 | tf_op jit(solution)/shard_map/ppermute | solution.py:155
  357.6 6.1 %collective-permute-done.11 = bf16[8,2048]{1,0:T(8,128)(2,1)S(1)} collective-permute-done((bf16[8,2048]{1,0:T(8,128)(2,1)S(1)}, bf16[8,2048]{1,0:T(8,128)(2,1)S(1)}, u32[]{:S(2)}, u32[]{:S(2)}) %collective-permute-start.11) | collective-permute-done | bytes 32800 | tf_op jit(solution)/shard_map/ppermute | solution.py:155
  363.7 0.2 reduce-window.4
  363.9 5.9 %collective-permute-done.12 = bf16[8,2048]{1,0:T(8,128)(2,1)S(1)} collective-permute-done((bf16[8,2048]{1,0:T(8,128)(2,1)S(1)}, bf16[8,2048]{1,0:T(8,128)(2,1)S(1)}, u32[]{:S(2)}, u32[]{:S(2)}) %collective-permute-start.12) | collective-permute-done | bytes 32800 | tf_op jit(solution)/shard_map/ppermute | solution.py:155
  369.8 0.6 slice_bitcast_fusion
  370.4 5.5 collective-permute-done.13
  375.9 0.5 iota_add_fusion
  376.5 5.6 %collective-permute-done.14 = bf16[8,2048]{1,0:T(8,128)(2,1)} collective-permute-done((bf16[8,2048]{1,0:T(8,128)(2,1)S(1)}, bf16[8,2048]{1,0:T(8,128)(2,1)}, u32[]{:S(2)}, u32[]{:S(2)}) %collective-permute-start.14) | collective-permute-done | bytes 32800 | tf_op jit(solution)/shard_map/ppermute | solution.py:155
  382.1 0.8 constant_dynamic-update-slice_fusion.31
  382.8 0.8 constant_dynamic-update-slice_fusion.30
  383.6 0.8 constant_dynamic-update-slice_fusion.29
  384.3 0.8 constant_dynamic-update-slice_fusion.28
  385.2 0.8 constant_dynamic-update-slice_fusion.15
  386.0 0.8 constant_dynamic-update-slice_fusion.14
  386.8 0.8 constant_dynamic-update-slice_fusion.13
  387.5 0.8 constant_dynamic-update-slice_fusion.12
  388.4 0.2 fusion.9
  388.6 1.0 fusion.7
  389.6 19.1 %collective-permute-start.15 = (bf16[128,2048]{1,0:T(8,128)(2,1)}, bf16[128,2048]{1,0:T(8,128)(2,1)}, u32[]{:S(2)}, u32[]{:S(2)}) collective-permute-start(bf16[128,2048]{1,0:T(8,128)(2,1)} %fusion.7), channel_id=1, source_target_pairs={{0,64},{64,0},{1,65},{65,1},{2,66},{66,2},{3,67},{67,3},{4,68},{68... | collective-permute-start | bytes 1572872 | tf_op jit(solution)/shard_map/ppermute | solution.py:24
  408.8 0.7 convert_element_type.137
  409.6 2.2 fusion.6
  411.8 1.4 broadcast_select_fusion.1
  413.2 5.7 %fusion.12 = f32[256,2048]{1,0:T(8,128)S(1)} fusion(bf16[2048,2048]{1,0:T(8,128)(2,1)} %param.29, bf16[128,2048]{1,0:T(8,128)(2,1)S(1)} %get-tuple-element.8, bf16[128,2048]{1,0:T(8,128)(2,1)S(1)} %get-tuple-element.7), kind=kOutput, calls=%fused_computation.22 | convolution fusion | flops 2149580800 | bytes 11534336 | tf_op jit(solution)/shard_map/dot_general | solution.py:170
  419.0 0.4 fusion.56
  419.4 62.7 %pmax.7 = f32[128]{0:T(128)S(1)} all-reduce(f32[128]{0:T(128)S(1)} %get-tuple-element.3), channel_id=1, replica_groups=mesh['guide'=2,'tensor'=16,'batch'=4] {'guide','tensor'}, use_global_device_ids=true, to_apply=%region_11.12 | all-reduce | flops 128 | bytes 1024 | tf_op jit(solution)/shard_map/pmax | solution.py:184
  482.1 0.3 exponential_reduce_fusion
  482.4 65.3 %psum.7 = f32[128]{0:T(128)S(1)} all-reduce(f32[128]{0:T(128)S(1)} %exponential_reduce_fusion), channel_id=1, replica_groups=mesh['guide'=2,'tensor'=16,'batch'=4] {'guide','tensor'}, use_global_device_ids=true, to_apply=%region_13.14 | all-reduce | flops 128 | bytes 1024 | tf_op jit(solution)/shard_map/psum | solution.py:185
  547.7 1.1 subtract_subtract_fusion
  (95 shorter events, 1.4 us)
Async XLA Ops:
  7.2 189.4 %copy-start = (bf16[512,2048]{1,0:T(8,128)(2,1)S(1)}, bf16[512,2048]{1,0:T(8,128)(2,1)}, u32[]{:S(2)}) copy-start(bf16[512,2048]{1,0:T(8,128)(2,1)} %param.27) | copy-start | bytes 6291460
  7.2 28.9 %copy-start.8 = (s32[1,8]{1,0:T(1,128)S(1)}, s32[1,8]{1,0:T(1,128)}, u32[]{:S(2)}) copy-start(s32[1,8]{1,0:T(1,128)} %param.22) | copy-start | bytes 100
  31.3 27.8 %all-to-all-start = ((bf16[16,8,192]{2,1,0:T(8,128)(2,1)}), bf16[16,8,192]{2,1,0:T(8,128)(2,1)S(1)}, u32[]{:S(2)}, u32[]{:S(2)}) async-start(bf16[16,8,192]{2,1,0:T(8,128)(2,1)} %bitcast.3), calls=%async_computation | async-start | bytes 131072 | tf_op jit(solution)/shard_map/all_to_all | solution.py:131
  36.0 140.1 %all-reduce.5.cloned.1.call-start = ((), (), s32[]{:S(2)}) async-start(), calls=%async_computation.2 | async-start | bytes 1048576
  65.5 21.1 %copy-start.13 = (u32[128]{0:T(128)S(1)}, u32[128]{0:T(128)}, u32[]{:S(2)}) copy-start(u32[128]{0:T(128)} %constant.96) | copy-start | bytes 1540
  65.5 110.6 %copy-start.1 = (bf16[1,8,2048]{2,1,0:T(8,128)(2,1)S(1)}, bf16[1,8,2048]{2,1,0:T(8,128)(2,1)}, u32[]{:S(2)}) copy-start(bf16[1,8,2048]{2,1,0:T(8,128)(2,1)} %param.17) | copy-start | bytes 98308
  65.5 111.5 %copy-start.7 = (f32[2048]{0:T(1024)S(1)}, f32[2048]{0:T(1024)}, u32[]{:S(2)}) copy-start(f32[2048]{0:T(1024)} %param.24) | copy-start | bytes 24580
  86.5 202.9 %all-reduce.7.cloned.1.call-start = ((), (), s32[]{:S(2)}) async-start(), calls=%async_computation.3 | async-start | bytes 1048576
  196.6 167.1 %copy-start.10 = (s32[4]{0:T(128)S(1)}, s32[4]{0:T(128)}, u32[]{:S(2)}) copy-start(s32[4]{0:T(128)} %param.32) | copy-start | bytes 52
  199.8 188.8 %copy-start.6 = (f32[2048]{0:T(1024)S(1)}, f32[2048]{0:T(1024)}, u32[]{:S(2)}) copy-start(f32[2048]{0:T(1024)} %param.28) | copy-start | bytes 24580
  199.8 209.8 %copy-start.9 = (f32[2048]{0:T(1024)S(1)}, f32[2048]{0:T(1024)}, u32[]{:S(2)}) copy-start(f32[2048]{0:T(1024)} %param.30) | copy-start | bytes 24580
  290.2 121.6 %copy-start.2 = (bf16[8,2048]{1,0:T(8,128)(2,1)}, bf16[8,2048]{1,0:T(8,128)(2,1)S(1)}, u32[]{:S(2)}) copy-start(bf16[8,2048]{1,0:T(8,128)(2,1)S(1)} %fusion.39) | copy-start | bytes 98308
  290.2 6.2 %collective-permute-start = (bf16[8,2048]{1,0:T(8,128)(2,1)S(1)}, bf16[8,2048]{1,0:T(8,128)(2,1)S(1)}, u32[]{:S(2)}, u32[]{:S(2)}) collective-permute-start(bf16[8,2048]{1,0:T(8,128)(2,1)S(1)} %fusion.39), channel_id=1, source_target_pairs={{0,4},{4,8},{8,12},{12,16},{16,20},{20,24},{24,28},{28,32},{32,36}... | collective-permute-start | bytes 98312 | tf_op jit(solution)/shard_map/ppermute | solution.py:155
  296.4 6.1 %collective-permute-start.1 = (bf16[8,2048]{1,0:T(8,128)(2,1)S(1)}, bf16[8,2048]{1,0:T(8,128)(2,1)S(1)}, u32[]{:S(2)}, u32[]{:S(2)}) collective-permute-start(bf16[8,2048]{1,0:T(8,128)(2,1)S(1)} %collective-permute-done), channel_id=1, source_target_pairs={{0,4},{4,8},{8,12},{12,16},{16,20},{20,24},{24,28},{28,32},{32,36}... | collective-permute-start | bytes 98312 | tf_op jit(solution)/shard_map/ppermute | solution.py:155
  302.4 6.1 %collective-permute-start.2 = (bf16[8,2048]{1,0:T(8,128)(2,1)S(1)}, bf16[8,2048]{1,0:T(8,128)(2,1)S(1)}, u32[]{:S(2)}, u32[]{:S(2)}) collective-permute-start(bf16[8,2048]{1,0:T(8,128)(2,1)S(1)} %collective-permute-done.1), channel_id=1, source_target_pairs={{0,4},{4,8},{8,12},{12,16},{16,20},{20,24},{24,28},{28,32},{32,36}... | collective-permute-start | bytes 98312 | tf_op jit(solution)/shard_map/ppermute | solution.py:155
  308.5 6.1 %collective-permute-start.3 = (bf16[8,2048]{1,0:T(8,128)(2,1)S(1)}, bf16[8,2048]{1,0:T(8,128)(2,1)S(1)}, u32[]{:S(2)}, u32[]{:S(2)}) collective-permute-start(bf16[8,2048]{1,0:T(8,128)(2,1)S(1)} %collective-permute-done.2), channel_id=1, source_target_pairs={{0,4},{4,8},{8,12},{12,16},{16,20},{20,24},{24,28},{28,32},{32,36}... | collective-permute-start | bytes 98312 | tf_op jit(solution)/shard_map/ppermute | solution.py:155
  314.6 6.5 %collective-permute-start.4 = (bf16[8,2048]{1,0:T(8,128)(2,1)S(1)}, bf16[8,2048]{1,0:T(8,128)(2,1)S(1)}, u32[]{:S(2)}, u32[]{:S(2)}) collective-permute-start(bf16[8,2048]{1,0:T(8,128)(2,1)S(1)} %collective-permute-done.3), channel_id=1, source_target_pairs={{0,4},{4,8},{8,12},{12,16},{16,20},{20,24},{24,28},{28,32},{32,36}... | collective-permute-start | bytes 98312 | tf_op jit(solution)/shard_map/ppermute | solution.py:155
  321.1 6.1 %collective-permute-start.5 = (bf16[8,2048]{1,0:T(8,128)(2,1)S(1)}, bf16[8,2048]{1,0:T(8,128)(2,1)S(1)}, u32[]{:S(2)}, u32[]{:S(2)}) collective-permute-start(bf16[8,2048]{1,0:T(8,128)(2,1)S(1)} %collective-permute-done.4), channel_id=1, source_target_pairs={{0,4},{4,8},{8,12},{12,16},{16,20},{20,24},{24,28},{28,32},{32,36}... | collective-permute-start | bytes 98312 | tf_op jit(solution)/shard_map/ppermute | solution.py:155
  327.2 6.1 %collective-permute-start.6 = (bf16[8,2048]{1,0:T(8,128)(2,1)S(1)}, bf16[8,2048]{1,0:T(8,128)(2,1)S(1)}, u32[]{:S(2)}, u32[]{:S(2)}) collective-permute-start(bf16[8,2048]{1,0:T(8,128)(2,1)S(1)} %collective-permute-done.5), channel_id=1, source_target_pairs={{0,4},{4,8},{8,12},{12,16},{16,20},{20,24},{24,28},{28,32},{32,36}... | collective-permute-start | bytes 98312 | tf_op jit(solution)/shard_map/ppermute | solution.py:155
  333.3 6.1 %collective-permute-start.7 = (bf16[8,2048]{1,0:T(8,128)(2,1)S(1)}, bf16[8,2048]{1,0:T(8,128)(2,1)S(1)}, u32[]{:S(2)}, u32[]{:S(2)}) collective-permute-start(bf16[8,2048]{1,0:T(8,128)(2,1)S(1)} %collective-permute-done.6), channel_id=1, source_target_pairs={{0,4},{4,8},{8,12},{12,16},{16,20},{20,24},{24,28},{28,32},{32,36}... | collective-permute-start | bytes 98312 | tf_op jit(solution)/shard_map/ppermute | solution.py:155
  339.3 6.1 %collective-permute-start.8 = (bf16[8,2048]{1,0:T(8,128)(2,1)S(1)}, bf16[8,2048]{1,0:T(8,128)(2,1)S(1)}, u32[]{:S(2)}, u32[]{:S(2)}) collective-permute-start(bf16[8,2048]{1,0:T(8,128)(2,1)S(1)} %collective-permute-done.7), channel_id=1, source_target_pairs={{0,4},{4,8},{8,12},{12,16},{16,20},{20,24},{24,28},{28,32},{32,36}... | collective-permute-start | bytes 98312 | tf_op jit(solution)/shard_map/ppermute | solution.py:155
  345.4 6.1 %collective-permute-start.9 = (bf16[8,2048]{1,0:T(8,128)(2,1)S(1)}, bf16[8,2048]{1,0:T(8,128)(2,1)S(1)}, u32[]{:S(2)}, u32[]{:S(2)}) collective-permute-start(bf16[8,2048]{1,0:T(8,128)(2,1)S(1)} %collective-permute-done.8), channel_id=1, source_target_pairs={{0,4},{4,8},{8,12},{12,16},{16,20},{20,24},{24,28},{28,32},{32,36}... | collective-permute-start | bytes 98312 | tf_op jit(solution)/shard_map/ppermute | solution.py:155
  351.5 6.1 %collective-permute-start.10 = (bf16[8,2048]{1,0:T(8,128)(2,1)S(1)}, bf16[8,2048]{1,0:T(8,128)(2,1)S(1)}, u32[]{:S(2)}, u32[]{:S(2)}) collective-permute-start(bf16[8,2048]{1,0:T(8,128)(2,1)S(1)} %collective-permute-done.9), channel_id=1, source_target_pairs={{0,4},{4,8},{8,12},{12,16},{16,20},{20,24},{24,28},{28,32},{32,36}... | collective-permute-start | bytes 98312 | tf_op jit(solution)/shard_map/ppermute | solution.py:155
  357.6 6.1 %collective-permute-start.11 = (bf16[8,2048]{1,0:T(8,128)(2,1)S(1)}, bf16[8,2048]{1,0:T(8,128)(2,1)S(1)}, u32[]{:S(2)}, u32[]{:S(2)}) collective-permute-start(bf16[8,2048]{1,0:T(8,128)(2,1)S(1)} %collective-permute-done.10), channel_id=1, source_target_pairs={{0,4},{4,8},{8,12},{12,16},{16,20},{20,24},{24,28},{28,32},{32,36}... | collective-permute-start | bytes 98312 | tf_op jit(solution)/shard_map/ppermute | solution.py:155
  363.7 12.7 %copy-start.3 = (bf16[8,2048]{1,0:T(8,128)(2,1)}, bf16[8,2048]{1,0:T(8,128)(2,1)S(1)}, u32[]{:S(2)}) copy-start(bf16[8,2048]{1,0:T(8,128)(2,1)S(1)} %collective-permute-done.11) | copy-start | bytes 98308
  363.7 6.1 %collective-permute-start.12 = (bf16[8,2048]{1,0:T(8,128)(2,1)S(1)}, bf16[8,2048]{1,0:T(8,128)(2,1)S(1)}, u32[]{:S(2)}, u32[]{:S(2)}) collective-permute-start(bf16[8,2048]{1,0:T(8,128)(2,1)S(1)} %collective-permute-done.11), channel_id=1, source_target_pairs={{0,4},{4,8},{8,12},{12,16},{16,20},{20,24},{24,28},{28,32},{32,36}... | collective-permute-start | bytes 98312 | tf_op jit(solution)/shard_map/ppermute | solution.py:155
  369.8 6.6 %copy-start.4 = (bf16[8,2048]{1,0:T(8,128)(2,1)}, bf16[8,2048]{1,0:T(8,128)(2,1)S(1)}, u32[]{:S(2)}) copy-start(bf16[8,2048]{1,0:T(8,128)(2,1)S(1)} %collective-permute-done.12) | copy-start | bytes 98308
  369.8 6.1 %collective-permute-start.13 = (bf16[8,2048]{1,0:T(8,128)(2,1)S(1)}, bf16[8,2048]{1,0:T(8,128)(2,1)S(1)}, u32[]{:S(2)}, u32[]{:S(2)}) collective-permute-start(bf16[8,2048]{1,0:T(8,128)(2,1)S(1)} %collective-permute-done.12), channel_id=1, source_target_pairs={{0,4},{4,8},{8,12},{12,16},{16,20},{20,24},{24,28},{28,32},{32,36}... | collective-permute-start | bytes 98312 | tf_op jit(solution)/shard_map/ppermute | solution.py:155
  375.9 0.6 copy-start.5
  375.9 6.2 %collective-permute-start.14 = (bf16[8,2048]{1,0:T(8,128)(2,1)S(1)}, bf16[8,2048]{1,0:T(8,128)(2,1)}, u32[]{:S(2)}, u32[]{:S(2)}) collective-permute-start(bf16[8,2048]{1,0:T(8,128)(2,1)S(1)} %collective-permute-done.13), channel_id=1, source_target_pairs={{0,4},{4,8},{8,12},{12,16},{16,20},{20,24},{24,28},{28,32},{32,36}... | collective-permute-start | bytes 98312 | tf_op jit(solution)/shard_map/ppermute | solution.py:155
  376.5 32.3 %copy-start.11 = (s32[3]{0:T(128)S(1)}, s32[3]{0:T(128)}, u32[]{:S(2)}) copy-start(s32[3]{0:T(128)} %slice_bitcast_fusion) | copy-start | bytes 40
  376.5 32.3 %copy-start.12 = (s32[128]{0:T(128)S(1)}, s32[128]{0:T(128)}, u32[]{:S(2)}) copy-start(s32[128]{0:T(128)} %iota_add_fusion) | copy-start | bytes 1540
  389.6 22.2 %collective-permute-start.15 = (bf16[128,2048]{1,0:T(8,128)(2,1)}, bf16[128,2048]{1,0:T(8,128)(2,1)}, u32[]{:S(2)}, u32[]{:S(2)}) collective-permute-start(bf16[128,2048]{1,0:T(8,128)(2,1)} %fusion.7), channel_id=1, source_target_pairs={{0,64},{64,0},{1,65},{65,1},{2,66},{66,2},{3,67},{67,3},{4,68},{68... | collective-permute-start | bytes 1572872 | tf_op jit(solution)/shard_map/ppermute | solution.py:24
Sparse Core Ops, SparseCore 0:
  86.7 89.4 all-reduce.4
  200.0 89.4 all-reduce.6
